TPU v7x, 32 devices: a whole 2x2x4 slice. The times are simulated.
32 devices in a mesh: ctx: 4 (over z), head: 4 (over x, core), rep: 2 (over y).
Axes of the slice: x: 2, y: 2, z: 4, core: 2. Of those that a mesh axis runs over, the one named last changes fastest.
Arguments:
- queries: bfloat16 [4, 256, 2048], P('rep', 'ctx', 'head'), may hold values from -6 to 6
- keyvals: bfloat16 [4, 256, 4, 128], P('rep', 'ctx', 'head'), may hold values from -6 to 6
- sinks: float32 [32], P('head'), may hold values from -1 to 3
- stream: bfloat16 [4, 256, 2880], P('rep', 'ctx', 'head'), may hold values from -6 to 6
- out_weight: bfloat16 [2048, 2880], P('head', 'ctx'), may hold values from -0.75 to 0.75
- norm_gain: float32 [2880], replicated, may hold values from 0.1 to 1.9
- router: bfloat16 [2880, 32], replicated, may hold values from -0.12 to 0.12
- expert_ids: int32 [4, 256, 4], P('rep', 'ctx'), may hold values from 0 to 31, all different within a row; in each aligned block of 64 rows (0 to 63, 64 to 127, ..., all dimensions but the last counted through in order) at most 12 rows name the same one
- w_gate_up: bfloat16 [64, 720, 5760], P('ctx', 'head'), may hold values from -0.109375 to 0.109375
- w_down: bfloat16 [64, 720, 2880], P('ctx', None, 'head'), may hold values from -0.15625 to 0.15625
Outputs:
- layer_out: bfloat16 [4, 256, 2880], P('rep', 'ctx', 'head')
Inputs may be any that keep to these rules, and one draw needn't show every extreme that they name: `expert_ids`: each position names 4 different experts. Within each aligned block of 64 positions of a sequence no expert is named by more than 12 positions, and in every draw some block has an expert named by exactly 12.
All inputs are finite; a program needn't handle non-finite values.
Results may differ from a plain program's by a relative error of at most 0.015.
Values may be sent and summed in bfloat16 or wider, within the bound.
A program may use at most 192 MiB of HBM per device.

v0:
```python
import jax
import jax.numpy as jnp
from jax import lax
from jax.sharding import PartitionSpec as P


def on_device(
    queries, keyvals, sinks, stream, out_weight, norm_gain, router, expert_ids, w_gate_up, w_down
):
    ctx_count = lax.axis_size("ctx")
    rep_count = lax.axis_size("rep")
    local_seqs = queries.shape[0]
    tokens = queries.shape[1]
    row_count = local_seqs * tokens
    kv_local = keyvals.shape[2]
    head_dim = keyvals.shape[3] // 2
    q_local = queries.shape[2] // head_dim
    query_group_size = q_local // kv_local
    wide_rows = query_group_size * tokens
    col_width = stream.shape[2]
    first_pos = lax.axis_index("ctx") * tokens
    last_pos = first_pos + tokens - 1
    score_scale = head_dim ** (-0.5)
    scaled_queries = queries * jnp.asarray(score_scale, jnp.bfloat16)
    query_grid = scaled_queries.reshape(local_seqs, tokens, kv_local, query_group_size, head_dim)
    query_wide = jnp.transpose(query_grid, (0, 2, 3, 1, 4)).reshape(
        local_seqs, kv_local, wide_rows, head_dim
    )
    positions = first_pos + jnp.tile(jnp.arange(tokens), query_group_size)
    sink_rows = jnp.repeat(sinks.reshape(kv_local, query_group_size), tokens, axis=1)
    sink_grid = jnp.broadcast_to(sink_rows[None], (local_seqs, kv_local, wide_rows))
    start_state = (
        sink_grid,
        jnp.ones_like(sink_grid),
        jnp.zeros((local_seqs, kv_local, head_dim, wide_rows), jnp.float32),
    )
    gate_up_weights = w_gate_up.reshape(
        w_gate_up.shape[0], w_gate_up.shape[1], 2, w_gate_up.shape[2] // 2
    )

    def attend_block(running, shard_piece):
        peak_old, denom_old, accum_old = running
        key_block = shard_piece[..., :head_dim]
        value_block = shard_piece[..., head_dim:]
        scores = jnp.einsum(
            "skmd,snkd->sknm", query_wide, key_block, preferred_element_type=jnp.float32
        )
        key_pos = jnp.arange(shard_piece.shape[1])
        visible = key_pos[:, None] <= positions[None, :]
        masked = jnp.where(visible[None, None], scores, -jnp.inf)
        peak_new = jnp.maximum(peak_old, jnp.max(masked, axis=2))
        exp_terms = jnp.exp(masked - peak_new[:, :, None, :])
        factor = jnp.exp(peak_old - peak_new)
        denom_new = denom_old * factor + jnp.sum(exp_terms, axis=2)
        accum_new = accum_old * factor[:, :, None, :] + jnp.einsum(
            "sknm,snkd->skdm",
            exp_terms.astype(jnp.bfloat16),
            value_block,
            preferred_element_type=jnp.float32,
        )
        return (peak_new, denom_new, accum_new)

    shard_piece = lax.all_gather(keyvals, "ctx", axis=1, tiled=True)

    def keep_state(state_in):
        return state_in

    def update_state(state_in):
        return attend_block(state_in, shard_piece)

    peak_fin, denom_fin, accum_fin = lax.cond(
        jnp.int32(0) > last_pos, keep_state, update_state, start_state
    )
    normalized = (accum_fin / denom_fin[:, :, None, :]).reshape(
        local_seqs, kv_local, head_dim, query_group_size, tokens
    )
    attended = (
        jnp.transpose(normalized, (0, 4, 1, 3, 2))
        .reshape(row_count, q_local * head_dim)
        .astype(jnp.bfloat16)
    )
    partial_proj = jnp.dot(
        attended,
        lax.all_gather(out_weight, "ctx", axis=1, tiled=True),
        preferred_element_type=jnp.float32,
    )
    col_start = lax.axis_index("head") * col_width
    own_stream = stream.reshape(row_count, col_width).astype(jnp.float32)
    own_cols = lax.dynamic_slice_in_dim(partial_proj, col_start, col_width, 1) + own_stream
    placed = lax.dynamic_update_slice_in_dim(partial_proj, own_cols, col_start, 1)
    hidden_state = lax.psum(placed.astype(jnp.bfloat16), "head")
    state_float = hidden_state.astype(jnp.float32)
    inverse = lax.rsqrt(jnp.mean(state_float * state_float, axis=-1, keepdims=True) + 1e-05)
    send_rows = (state_float * inverse * norm_gain).astype(jnp.bfloat16)
    logits = jnp.dot(send_rows, router, preferred_element_type=jnp.float32)
    own_state = lax.dynamic_slice_in_dim(hidden_state, col_start, col_width, 1)
    expert_rows = expert_ids.reshape(row_count, expert_ids.shape[2])
    expert_count = router.shape[1]
    top_count = expert_rows.shape[1]
    member = expert_rows[:, :, None] == jnp.arange(expert_count)[None, None, :]
    chosen = jnp.sum(jnp.where(member, logits[:, None, :], 0.0), axis=-1)
    mix_weights = jax.nn.softmax(chosen, axis=-1)
    block_rows = row_count // rep_count
    member_int = member.astype(jnp.int32).reshape(rep_count, block_rows * top_count, expert_count)
    earlier = jnp.cumsum(member_int, axis=1) - member_int
    slot_rank = jnp.sum(earlier * member_int, axis=-1).reshape(row_count, top_count)
    target_rep = (jnp.arange(row_count) // block_rows)[:, None]
    local_halves = w_gate_up.shape[0]
    capacity = 3 * tokens // 16
    slot_total = ctx_count * rep_count * local_halves * capacity
    slot_lists = []
    for half_index in range(2):
        weight_row = 2 * expert_rows + half_index
        target_rank = weight_row // local_halves * rep_count + target_rep
        slot_lists.append(
            (target_rank * local_halves + weight_row % local_halves) * capacity + slot_rank
        )
    slot_index = jnp.stack(slot_lists, axis=-1)
    row_ids = jnp.broadcast_to(jnp.arange(row_count)[:, None, None], slot_index.shape)
    spread = (
        jnp.zeros((slot_total, row_count), jnp.bfloat16)
        .at[slot_index.reshape(-1), row_ids.reshape(-1)]
        .set(1.0)
    )
    outgoing = jnp.dot(spread, send_rows, preferred_element_type=jnp.float32).astype(jnp.bfloat16)
    outgoing = outgoing.reshape(ctx_count * rep_count, local_halves, capacity, send_rows.shape[1])
    gate_up = jnp.einsum(
        "sgcd,ghzd->sgczh",
        lax.all_to_all(outgoing, ("ctx", "rep"), split_axis=0, concat_axis=0, tiled=True),
        gate_up_weights,
        preferred_element_type=jnp.float32,
    )
    gate_part = gate_up[:, :, :, 0]
    up_part = gate_up[:, :, :, 1]
    active = (gate_part * jax.nn.sigmoid(1.702 * gate_part) * (up_part + 1.0)).astype(jnp.bfloat16)
    expert_out = jnp.einsum(
        "sgch,ghd->sgcd",
        lax.all_gather(active, "head", axis=3, tiled=True),
        w_down,
        preferred_element_type=jnp.float32,
    ).astype(jnp.bfloat16)
    returned = lax.all_to_all(expert_out, ("ctx", "rep"), split_axis=0, concat_axis=0, tiled=True)
    returned_rows = returned.reshape(slot_total, col_width)
    picked_rows = returned_rows[slot_index]
    combined = jnp.sum(mix_weights[:, :, None, None] * picked_rows.astype(jnp.float32), axis=(1, 2))
    layer_out = (own_state.astype(jnp.float32) + combined).astype(jnp.bfloat16)
    return layer_out.reshape(local_seqs, tokens, col_width)


def solution(mesh):
    placed = (
        P("rep", "ctx", "head"),
        P("rep", "ctx", "head", None),
        P("head"),
        P("rep", "ctx", "head"),
        P("head", "ctx"),
        P(),
        P(),
        P("rep", "ctx", None),
        P("ctx", "head", None),
        P("ctx", None, "head"),
    )
    return jax.shard_map(
        on_device, mesh=mesh, in_specs=placed, out_specs=P("rep", "ctx", "head"), check_vma=False
    )
```

profile of v0, /device:TPU:0, one launch (start us, length us, event | category | flops | bytes accessed | tf_op | source)
XLA Modules:
  0.0 661.9 jit_solution(3322971049654471776)
XLA Ops:
  12.8 16.1 %all_gather.9 = bf16[2,256,1,128]{3,0,2,1:T(2,128)(2,1)S(1)} all-gather(bf16[2,64,1,128]{3,0,2,1:T(2,128)(2,1)S(1)} %copy.70), channel_id=1, replica_groups=mesh['ctx'=4,'head'=4,'rep'=2] {'ctx'}, dimensions={1}, use_global_device_ids=true | all-gather | bytes 163840 | tf_op jit(solution)/shard_map/all_gather | solution.py:63
  33.0 39.7 %all-gather.3.cloned.1.call-done = bf16[512,2880]{0,1:T(8,128)(2,1)} async-done(((bf16[512,720]{0,1:T(8,128)(2,1)}), bf16[512,2880]{0,1:T(8,128)(2,1)}) %all-gather.3.cloned.1.call-update) | async-done | bytes 2949136 | tf_op jit(solution)/shard_map/all_gather | solution.py:84
  72.8 2.8 fusion.54
  76.8 8.2 %scatter_custom_fusion = bf16[196608]{0:T(1024)(128)(2,1)S(1)} fusion(s32[1024]{0:T(1024)S(1)} %broadcast_select_fusion, bf16[1024]{0:T(1024)(128)(2,1)S(1)} %broadcast.896, bf16[]{:T(256)} %constant.105.clone.1), kind=kCustom, calls=%fused_computation.44 | custom fusion | bytes 393218
  85.1 24.8 %all-reduce.2.cloned.1.call-done = bf16[128,2880]{0,1:T(8,128)(2,1)} async-done(((bf16[128,2880]{0,1:T(8,128)(2,1)}), bf16[128,2880]{0,1:T(8,128)(2,1)}) %all-reduce.2.cloned.1.call-update) | async-done | bytes 737296 | tf_op jit(solution)/shard_map/psum | solution.py:91
  111.4 7.0 %convolution_convert_fusion = bf16[1536,2880]{0,1:T(8,128)(2,1)} fusion(bf16[196608]{0:T(1024)(128)(2,1)S(1)} %scatter_custom_fusion, bf16[128,2880]{0,1:T(8,128)(2,1)} %all-reduce.2.cloned.1.call-done, f32[2880]{0:T(1024)S(1)} %copy-done.4, f32[128]{0:T(128)S(1)} %add_rsqrt_fusion), kind=kOutput, calls=%fused_computation.24 | convolution fusion | flops 1138360320 | bytes 9989888 | tf_op jit(solution)/shard_map/dot_general | solution.py:125
  118.5 12.5 %copy.84 = bf16[1536,2880]{1,0:T(8,128)(2,1)} copy(bf16[1536,2880]{0,1:T(8,128)(2,1)} %convolution_convert_fusion) | data formatting | bytes 17694720 | tf_op jit(solution)/shard_map/convert_element_type | solution.py:125
  131.0 13.4 %reshape.727 = bf16[8,16,12,2880]{3,2,1,0:T(8,128)(2,1)} reshape(bf16[1536,2880]{1,0:T(8,128)(2,1)} %copy.84) | data formatting | bytes 17694720 | tf_op jit(solution)/shard_map/reshape | solution.py:126
  144.4 9.7 %copy.85 = bf16[8,16,12,2880]{3,1,2,0:T(8,128)(2,1)} copy(bf16[8,16,12,2880]{3,2,1,0:T(8,128)(2,1)} %reshape.727) | data formatting | bytes 17694720 | tf_op jit(solution)/shard_map/reshape | solution.py:126
  154.1 5.5 all-to-all-start
  159.7 55.8 %reshape.728 = bf16[16,180,2,2880]{3,2,0,1:T(2,128)(2,1)} reshape(bf16[16,180,5760]{2,0,1:T(8,128)(2,1)} %param.20) | data formatting | bytes 66355200 | tf_op jit(solution)/shard_map/reshape | solution.py:37
  215.5 140.7 %all-to-all-done = bf16[8,16,12,2880]{3,1,2,0:T(8,128)(2,1)} async-done(((bf16[8,16,12,2880]{3,1,2,0:T(8,128)(2,1)}), bf16[8,16,12,2880]{3,1,2,0:T(8,128)(2,1)}, u32[]{:S(2)}, u32[]{:S(2)}) %all-to-all-start) | async-done | bytes 8847392 | tf_op jit(solution)/shard_map/all_to_all | solution.py:129
  356.1 43.2 %fusion.14 = f32[8,16,12,2,180]{4,2,3,0,1:T(8,128)S(1)} fusion(bf16[16,180,2,2880,1]{3,2,0,1,4:T(2,128)(2,1)} %bitcast.104, bf16[8,16,12,2880,1]{3,1,2,0,4:T(8,128)(2,1)} %bitcast.12), kind=kOutput, calls=%fused_computation.27 | convolution fusion | flops 3185049600 | bytes 44236800 | tf_op jit(solution)/shard_map/sgcd,ghzd->sgczh/dot_general | solution.py:127
  401.0 15.0 %copy.89 = bf16[8,16,12,180]{1,0,2,3:T(8,128)(2,1)} copy(bf16[8,16,12,180]{3,2,0,1:T(8,128)(2,1)} %fusion.21) | data formatting | bytes 1105920 | tf_op jit(solution)/shard_map/convert_element_type | solution.py:135
  416.0 112.2 %all-gather.5.cloned.1.call-done = bf16[8,16,12,720]{1,0,2,3:T(8,128)(2,1)} async-done(((bf16[8,16,12,180]{1,0,2,3:T(8,128)(2,1)}), bf16[8,16,12,720]{1,0,2,3:T(8,128)(2,1)}) %all-gather.5.cloned.1.call-update) | async-done | bytes 2211856 | tf_op jit(solution)/shard_map/all_gather | solution.py:138
  528.2 34.0 %copy.90 = bf16[8,16,12,720]{3,2,0,1:T(8,128)(2,1)S(1)} copy(bf16[8,16,12,720]{1,0,2,3:T(8,128)(2,1)} %all-gather.5.cloned.1.call-done) | data formatting | bytes 4423680 | tf_op jit(solution)/shard_map/all_gather | solution.py:138
  562.3 8.8 %convert_bitcast_fusion = bf16[8,16,12,720]{3,2,0,1:T(8,128)(2,1)S(1)} fusion(bf16[8,16,12,720]{3,2,0,1:T(8,128)(2,1)S(1)} %copy.90, bf16[16,720,720]{2,1,0:T(8,128)(2,1)} %param.21), kind=kOutput, calls=%fused_computation.26 | convolution fusion | flops 1593630720 | bytes 21012480 | tf_op jit(solution)/shard_map/sgch,ghd->sgcd/dot_general | solution.py:136
  571.0 2.7 copy.91
  573.8 5.9 all-to-all-start.1
  583.0 50.9 %all-to-all-done.1 = bf16[8,16,12,720]{3,1,2,0:T(8,128)(2,1)S(1)} async-done(((bf16[8,16,12,720]{3,1,2,0:T(8,128)(2,1)}), bf16[8,16,12,720]{3,1,2,0:T(8,128)(2,1)S(1)}, u32[]{:S(2)}, u32[]{:S(2)}) %all-to-all-start.1) | async-done | bytes 2211872 | tf_op jit(solution)/shard_map/all_to_all | solution.py:142
  636.4 4.0 reshape.729
  640.4 5.2 gather_fusion
  645.7 3.5 reshape.751
  649.2 3.0 multiply_reduce_fusion
  (93 shorter events, 25.9 us)
Async XLA Ops:
  6.5 574.2 %copy-start = (bf16[2880,32]{0,1:T(8,128)(2,1)S(1)}, bf16[2880,32]{0,1:T(8,128)(2,1)}, u32[]{:S(2)}) copy-start(bf16[2880,32]{0,1:T(8,128)(2,1)} %param.18) | copy-start | bytes 552964
  6.5 66.2 %all-gather.3.cloned.1.call-start = ((), (), s32[]{:S(2)}) async-start(), calls=%async_computation.2 | async-start | bytes 3686400 | tf_op jit(solution)/shard_map/all_gather | solution.py:84
  7.3 102.7 %all-reduce.2.cloned.1.call-start = ((), (), s32[]{:S(2)}) async-start(), calls=%async_computation.3 | async-start | bytes 1474560 | tf_op jit(solution)/shard_map/psum | solution.py:91
  28.9 3.9 copy-start.2
  75.5 1.1 copy-start.7
  75.5 1.2 copy-start.6
  75.6 35.9 %copy-start.4 = (f32[2880]{0:T(1024)S(1)}, f32[2880]{0:T(1024)}, u32[]{:S(2)}) copy-start(f32[2880]{0:T(1024)} %param.17) | copy-start | bytes 34564
  111.4 7.1 %copy-start.5 = (f32[128]{0:T(128)}, f32[128]{0:T(128)S(1)}, u32[]{:S(2)}) copy-start(f32[128]{0:T(128)S(1)} %add_rsqrt_fusion) | copy-start | bytes 1540
  154.1 202.0 %all-to-all-start = ((bf16[8,16,12,2880]{3,1,2,0:T(8,128)(2,1)}), bf16[8,16,12,2880]{3,1,2,0:T(8,128)(2,1)}, u32[]{:S(2)}, u32[]{:S(2)}) async-start(bf16[8,16,12,2880]{3,1,2,0:T(8,128)(2,1)} %copy.85), calls=%async_computation | async-start | bytes 18087936 | tf_op jit(solution)/shard_map/all_to_all | solution.py:129
  159.7 368.6 %all-gather.5.cloned.1.call-start = ((), (), s32[]{:S(2)}) async-start(), calls=%async_computation.4 | async-start | bytes 22118400 | tf_op jit(solution)/shard_map/all_gather | solution.py:138
  573.8 5.9 copy-start.3
  573.8 7.0 %copy-start.1 = (bf16[128,2880]{0,1:T(8,128)(2,1)S(1)}, bf16[128,2880]{0,1:T(8,128)(2,1)}, u32[]{:S(2)}) copy-start(bf16[128,2880]{0,1:T(8,128)(2,1)} %all-reduce.2.cloned.1.call-done) | copy-start | bytes 2211844
  573.8 60.1 %all-to-all-start.1 = ((bf16[8,16,12,720]{3,1,2,0:T(8,128)(2,1)}), bf16[8,16,12,720]{3,1,2,0:T(8,128)(2,1)S(1)}, u32[]{:S(2)}, u32[]{:S(2)}) async-start(bf16[8,16,12,720]{3,1,2,0:T(8,128)(2,1)} %copy.91), calls=%async_computation.1 | async-start | bytes 4718592 | tf_op jit(solution)/shard_map/all_to_all | solution.py:142
Sparse Core Ops, SparseCore 0:
  8.9 63.8 all-gather.2
  76.7 33.1 all-reduce.1
  416.1 112.0 all-gather.4
where the time goes:
time: 671 us; the launch traced here: 662 us
  waiting for transfers between devices  369 us (55%)
  local copies, waits for them, and re-layouts  175 us (26%)
  matrix products  63.7 us (9%)
  blocking collectives  16.1 us (2%)
  between operations  13.7 us (2%)
  other arithmetic  12.4 us (2%)
  starting transfers between devices  11.5 us (2%)
    all_to_all x1, waiting for transfers between devices, on_device(): lax.all_to_all(outgoing, ('ctx', 'rep'), split_axis=0, concat_axis=0, til...  141 us
    all_gather x1, waiting for transfers between devices, on_device(): lax.all_gather(active, 'head', axis=3, tiled=True)  112 us
    reshape x1, local copies, waits for them, and re-layouts, on_device(): w_gate_up.reshape(w_gate_up.shape[0], w_gate_up.shape[1], 2, w_gate_up.sh...  55.8 us
    all_to_all x1, waiting for transfers between devices, on_device(): lax.all_to_all(expert_out, ('ctx', 'rep'), split_axis=0, concat_axis=0, t...  50.9 us
    dot_general x1, matrix products, on_device(): jnp.einsum('sgcd,ghzd->sgczh', lax.all_to_all(outgoing, ('ctx', 'rep'), s...  43.2 us
    all_gather x1, waiting for transfers between devices, on_device(): lax.all_gather(out_weight, 'ctx', axis=1, tiled=True)  39.7 us
    all_gather x1, local copies, waits for them, and re-layouts, on_device(): lax.all_gather(active, 'head', axis=3, tiled=True)  34 us
    psum x1, waiting for transfers between devices, on_device(): hidden_state = lax.psum(placed.astype(jnp.bfloat16), 'head')  24.8 us
  transfers between devices with their start and end apart: 5, of which 5 were waited for; matrix products, arithmetic and copies ran while one was open for 12% of the time, Pallas kernels for 0%

commit v1 on v0

--- a/solution.py
+++ b/solution.py
@@ -2,6 +2,18 @@
 import jax.numpy as jnp
 from jax import lax
 from jax.sharding import PartitionSpec as P
+
+
+def gather_by_bits(x, axis, dim):
+    ways, here, step = (lax.axis_size(axis), lax.axis_index(axis), x.shape[dim])
+    line, have = (x, 1)
+    while have < ways:
+        line = jnp.concatenate(
+            [line, lax.ppermute(line, axis, [(d, (d - have) % ways) for d in range(ways)])],
+            axis=dim,
+        )
+        have = 2 * have
+    return jnp.roll(line, here * step, axis=dim)
 
 
 def on_device(
@@ -135,7 +147,7 @@
     active = (gate_part * jax.nn.sigmoid(1.702 * gate_part) * (up_part + 1.0)).astype(jnp.bfloat16)
     expert_out = jnp.einsum(
         "sgch,ghd->sgcd",
-        lax.all_gather(active, "head", axis=3, tiled=True),
+        gather_by_bits(active, "head", 3),
         w_down,
         preferred_element_type=jnp.float32,
     ).astype(jnp.bfloat16)

time: 671 us -> 568 us (0.85)
  waiting for transfers between devices: 369 us -> 285 us
  local copies, waits for them, and re-layouts: 175 us -> 153 us
    all_gather x1 -> x0, waiting for transfers between devices: 112 us -> none  [on_device(): lax.all_gather(active, 'head', axis=3, tiled=True)]
    ppermute x0 -> x2, waiting for transfers between devices: none -> 37.1 us  [gather_by_bits(): lax.ppermute(line, axis, [(d, (d - have) % ways) for d in range(ways)])]
    all_gather x1 -> x0, local copies, waits for them, and re-layouts: 34 us -> none  [on_device(): lax.all_gather(active, 'head', axis=3, tiled=True)]
    convert_element_type x1, local copies, waits for them, and re-layouts: 15 us -> 0.44 us  [on_device(): (gate_part * jax.nn.sigmoid(1.702 * gate_part) * (up_part + 1.0)).astype(...]
    concatenate x0 -> x2, local copies, waits for them, and re-layouts: none -> 12.2 us  [the longest x1 11.5 us: gather_by_bits(): return jnp.roll(line, here * step, axis=dim)]
    unnamed x21 -> x27, local copies, waits for them, and re-layouts: 9.86 us -> 21 us
    psum x1, waiting for transfers between devices: 24.8 us -> 13.6 us  [on_device(): hidden_state = lax.psum(placed.astype(jnp.bfloat16), 'head')]
  transfers between devices with their start and end apart: 5 -> 6, of which waited for: 5 -> 6; matrix products, arithmetic and copies ran while one was open for 12% -> 15% of each run, Pallas kernels for 0% -> 0%
where the time goes in v1:
time: 568 us; the launch traced here: 559 us
  waiting for transfers between devices  285 us (50%)
  local copies, waits for them, and re-layouts  153 us (27%)
  matrix products  66.7 us (12%)
  blocking collectives  15.9 us (3%)
  between operations  14.2 us (2%)
  other arithmetic  12.6 us (2%)
  starting transfers between devices  11.4 us (2%)
    all_to_all x1, waiting for transfers between devices, on_device(): lax.all_to_all(outgoing, ('ctx', 'rep'), split_axis=0, concat_axis=0, til...  141 us
    reshape x1, local copies, waits for them, and re-layouts, on_device(): w_gate_up.reshape(w_gate_up.shape[0], w_gate_up.shape[1], 2, w_gate_up.sh...  55.8 us
    all_to_all x1, waiting for transfers between devices, on_device(): lax.all_to_all(expert_out, ('ctx', 'rep'), split_axis=0, concat_axis=0, t...  50.8 us
    dot_general x1, matrix products, on_device(): jnp.einsum('sgcd,ghzd->sgczh', lax.all_to_all(outgoing, ('ctx', 'rep'), s...  45.2 us
    all_gather x1, waiting for transfers between devices, on_device(): lax.all_gather(out_weight, 'ctx', axis=1, tiled=True)  42.1 us
    ppermute x2, waiting for transfers between devices, gather_by_bits(): lax.ppermute(line, axis, [(d, (d - have) % ways) for d in range(ways)])  37.1 us
    reshape x2, local copies, waits for them, and re-layouts, on_device(): outgoing.reshape(ctx_count * rep_count, local_halves, capacity, send_rows...  23.2 us
    unnamed x27, local copies, waits for them, and re-layouts  21 us
  transfers between devices with their start and end apart: 6, of which 6 were waited for; matrix products, arithmetic and copies ran while one was open for 15% of the time, Pallas kernels for 0%

profile of v1, /device:TPU:0, one launch (start us, length us, event | category | flops | bytes accessed | tf_op | source)
XLA Modules:
  0.0 558.7 jit_solution(396669628054109797)
XLA Ops:
  12.0 15.9 %all_gather.6 = bf16[2,256,1,128]{3,0,2,1:T(2,128)(2,1)S(1)} all-gather(bf16[2,64,1,128]{3,0,2,1:T(2,128)(2,1)S(1)} %copy.75), channel_id=1, replica_groups=mesh['ctx'=4,'head'=4,'rep'=2] {'ctx'}, dimensions={1}, use_global_device_ids=true | all-gather | bytes 163840 | tf_op jit(solution)/shard_map/all_gather | solution.py:75
  30.6 42.1 %all-gather.2.cloned.1.call-done = bf16[512,2880]{0,1:T(8,128)(2,1)} async-done(((bf16[512,720]{0,1:T(8,128)(2,1)}), bf16[512,2880]{0,1:T(8,128)(2,1)}) %all-gather.2.cloned.1.call-update) | async-done | bytes 2949136 | tf_op jit(solution)/shard_map/all_gather | solution.py:96
  72.7 2.8 fusion.58
  76.8 19.6 %scatter_custom_fusion = bf16[196608]{0:T(1024)(128)(2,1)S(1)} fusion(s32[1024]{0:T(1024)S(1)} %broadcast_select_fusion, bf16[1024]{0:T(1024)(128)(2,1)S(1)} %broadcast.896, bf16[]{:T(256)} %constant.122.clone.1), kind=kCustom, calls=%fused_computation.46 | custom fusion | bytes 393218
  96.3 13.6 %all-reduce.2.cloned.1.call-done = bf16[128,2880]{0,1:T(8,128)(2,1)} async-done(((bf16[128,2880]{0,1:T(8,128)(2,1)}), bf16[128,2880]{0,1:T(8,128)(2,1)}) %all-reduce.2.cloned.1.call-update) | async-done | bytes 737296 | tf_op jit(solution)/shard_map/psum | solution.py:103
  111.5 7.0 %convolution_convert_fusion = bf16[1536,2880]{0,1:T(8,128)(2,1)} fusion(bf16[196608]{0:T(1024)(128)(2,1)S(1)} %scatter_custom_fusion, bf16[128,2880]{0,1:T(8,128)(2,1)} %all-reduce.2.cloned.1.call-done, f32[2880]{0:T(1024)S(1)} %copy-done.6, f32[128]{0:T(128)S(1)} %add_rsqrt_fusion), kind=kOutput, calls=%fused_computation.24 | convolution fusion | flops 1138360320 | bytes 9989888 | tf_op jit(solution)/shard_map/dot_general | solution.py:137
  118.6 12.5 %copy.89 = bf16[1536,2880]{1,0:T(8,128)(2,1)} copy(bf16[1536,2880]{0,1:T(8,128)(2,1)} %convolution_convert_fusion) | data formatting | bytes 17694720 | tf_op jit(solution)/shard_map/convert_element_type | solution.py:137
  131.0 13.4 %reshape.727 = bf16[8,16,12,2880]{3,2,1,0:T(8,128)(2,1)} reshape(bf16[1536,2880]{1,0:T(8,128)(2,1)} %copy.89) | data formatting | bytes 17694720 | tf_op jit(solution)/shard_map/reshape | solution.py:138
  144.5 9.8 %copy.90 = bf16[8,16,12,2880]{3,1,2,0:T(8,128)(2,1)} copy(bf16[8,16,12,2880]{3,2,1,0:T(8,128)(2,1)} %reshape.727) | data formatting | bytes 17694720 | tf_op jit(solution)/shard_map/reshape | solution.py:138
  154.3 5.5 all-to-all-start
  159.8 55.8 %reshape.728 = bf16[16,180,2,2880]{3,2,0,1:T(2,128)(2,1)} reshape(bf16[16,180,5760]{2,0,1:T(8,128)(2,1)} %param.20) | data formatting | bytes 66355200 | tf_op jit(solution)/shard_map/reshape | solution.py:49
  215.6 140.7 %all-to-all-done = bf16[8,16,12,2880]{3,1,2,0:T(8,128)(2,1)} async-done(((bf16[8,16,12,2880]{3,1,2,0:T(8,128)(2,1)}), bf16[8,16,12,2880]{3,1,2,0:T(8,128)(2,1)}, u32[]{:S(2)}, u32[]{:S(2)}) %all-to-all-start) | async-done | bytes 8847392 | tf_op jit(solution)/shard_map/all_to_all | solution.py:141
  356.3 45.2 %fusion.17 = f32[8,16,12,2,180]{4,2,3,0,1:T(8,128)} fusion(bf16[16,180,2,2880,1]{3,2,0,1,4:T(2,128)(2,1)} %bitcast.102, bf16[8,16,12,2880,1]{3,1,2,0,4:T(8,128)(2,1)} %bitcast.12), kind=kOutput, calls=%fused_computation.28 | convolution fusion | flops 3185049600 | bytes 44236800 | tf_op jit(solution)/shard_map/sgcd,ghzd->sgczh/dot_general | solution.py:139
  401.4 2.8 fusion.24
  405.0 9.5 %collective-permute-done = bf16[8,16,12,180]{3,1,2,0:T(8,128)(2,1)S(1)} collective-permute-done((bf16[8,16,12,180]{3,1,2,0:T(8,128)(2,1)S(1)}, bf16[8,16,12,180]{3,1,2,0:T(8,128)(2,1)S(1)}, u32[]{:S(2)}, u32[]{:S(2)}) %collective-permute-start) | collective-permute-done | bytes 552992 | tf_op jit(solution)/shard_map/ppermute | solution.py:12
  417.2 27.6 %collective-permute-done.1 = bf16[8,16,12,360]{3,1,2,0:T(8,128)(2,1)} collective-permute-done((bf16[8,16,12,360]{3,1,2,0:T(8,128)(2,1)S(1)}, bf16[8,16,12,360]{3,1,2,0:T(8,128)(2,1)}, u32[]{:S(2)}, u32[]{:S(2)}) %collective-permute-start.1) | collective-permute-done | bytes 1105952 | tf_op jit(solution)/shard_map/ppermute | solution.py:12
  447.5 11.5 %concatenate.34 = bf16[8,16,12,1440]{3,2,0,1:T(8,128)(2,1)} concatenate(bf16[8,16,12,180]{3,2,0,1:T(8,128)(2,1)S(1)} %fusion.24, bf16[8,16,12,180]{3,2,0,1:T(8,128)(2,1)S(1)} %copy.97, bf16[8,16,12,360]{3,2,0,1:T(8,128)(2,1)} %copy.98, bf16[8,16,12,180]{3,2,0,1:T(8,128)(2,1)S(1)} %fusion.24, bf16[8,16,12,180]{3,2,0,1:T(8,128)(2,1)S(1)} %copy.97, bf16[8,16,12,360]{3,2,0,1:T(8,128)(2,1)} %copy.98), dimensions={3} | concatenate | bytes 8847360 | tf_op jit(solution)/shard_map/jit(_roll_dynamic)/concatenate | solution.py:16
  459.0 9.8 %convert_bitcast_fusion = bf16[8,16,12,720]{3,2,0,1:T(8,128)(2,1)S(1)} fusion(bf16[16,720,720]{2,1,0:T(8,128)(2,1)} %param.21, bf16[8,16,12,1440]{3,2,0,1:T(8,128)(2,1)} %concatenate.34, s32[]{:T(128)S(6)} %select_n.172), kind=kOutput, calls=%fused_computation.26 | convolution fusion | flops 1593630720 | bytes 23052292 | tf_op jit(solution)/shard_map/sgch,ghd->sgcd/dot_general | solution.py:148
  471.6 4.5 all-to-all-start.1
  479.4 50.8 %all-to-all-done.1 = bf16[8,16,12,720]{3,1,2,0:T(8,128)(2,1)S(1)} async-done(((bf16[8,16,12,720]{3,1,2,0:T(8,128)(2,1)}), bf16[8,16,12,720]{3,1,2,0:T(8,128)(2,1)S(1)}, u32[]{:S(2)}, u32[]{:S(2)}) %all-to-all-start.1) | async-done | bytes 2211872 | tf_op jit(solution)/shard_map/all_to_all | solution.py:154
  532.8 4.0 reshape.729
  536.8 5.2 gather_fusion
  542.0 3.5 reshape.751
  545.5 3.0 multiply_reduce_fusion
  (104 shorter events, 30.1 us)
Async XLA Ops:
  6.5 471.4 %copy-start = (bf16[2880,32]{0,1:T(8,128)(2,1)S(1)}, bf16[2880,32]{0,1:T(8,128)(2,1)}, u32[]{:S(2)}) copy-start(bf16[2880,32]{0,1:T(8,128)(2,1)} %param.18) | copy-start | bytes 552964
  6.5 5.1 copy-start.3
  6.5 5.4 copy-start.5
  6.5 21.3 %copy-start.8 = (f32[8]{0:T(128)S(1)}, f32[8]{0:T(128)}, u32[]{:S(2)}) copy-start(f32[8]{0:T(128)} %param.14) | copy-start | bytes 100
  6.5 66.2 %all-gather.2.cloned.1.call-start = ((), (), s32[]{:S(2)}) async-start(), calls=%async_computation.2 | async-start | bytes 3686400 | tf_op jit(solution)/shard_map/all_gather | solution.py:96
  7.3 102.7 %all-reduce.2.cloned.1.call-start = ((), (), s32[]{:S(2)}) async-start(), calls=%async_computation.3 | async-start | bytes 1474560 | tf_op jit(solution)/shard_map/psum | solution.py:103
  27.9 2.5 copy-start.2
  75.5 1.1 copy-start.10
  75.5 1.2 copy-start.9
  75.5 36.0 %copy-start.6 = (f32[2880]{0:T(1024)S(1)}, f32[2880]{0:T(1024)}, u32[]{:S(2)}) copy-start(f32[2880]{0:T(1024)} %param.17) | copy-start | bytes 34564
  111.5 7.1 %copy-start.7 = (f32[128]{0:T(128)}, f32[128]{0:T(128)S(1)}, u32[]{:S(2)}) copy-start(f32[128]{0:T(128)S(1)} %add_rsqrt_fusion) | copy-start | bytes 1540
  154.3 202.0 %all-to-all-start = ((bf16[8,16,12,2880]{3,1,2,0:T(8,128)(2,1)}), bf16[8,16,12,2880]{3,1,2,0:T(8,128)(2,1)}, u32[]{:S(2)}, u32[]{:S(2)}) async-start(bf16[8,16,12,2880]{3,1,2,0:T(8,128)(2,1)} %copy.90), calls=%async_computation | async-start | bytes 18087936 | tf_op jit(solution)/shard_map/all_to_all | solution.py:141
  404.7 9.7 %collective-permute-start = (bf16[8,16,12,180]{3,1,2,0:T(8,128)(2,1)S(1)}, bf16[8,16,12,180]{3,1,2,0:T(8,128)(2,1)S(1)}, u32[]{:S(2)}, u32[]{:S(2)}) collective-permute-start(bf16[8,16,12,180]{3,1,2,0:T(8,128)(2,1)S(1)} %copy.94), channel_id=1, source_target_pairs={{0,6},{2,0},{4,2},{6,4},{1,7},{3,1},{5,3},{7,5},{8,14},{10,8},{12,... | collective-permute-start | bytes 1658888 | tf_op jit(solution)/shard_map/ppermute | solution.py:12
  416.1 28.7 %collective-permute-start.1 = (bf16[8,16,12,360]{3,1,2,0:T(8,128)(2,1)S(1)}, bf16[8,16,12,360]{3,1,2,0:T(8,128)(2,1)}, u32[]{:S(2)}, u32[]{:S(2)}) collective-permute-start(bf16[8,16,12,360]{3,1,2,0:T(8,128)(2,1)S(1)} %copy.96), channel_id=1, source_target_pairs={{0,4},{2,6},{4,0},{6,2},{1,5},{3,7},{5,1},{7,3},{8,12},{10,14},{12... | collective-permute-start | bytes 3317768 | tf_op jit(solution)/shard_map/ppermute | solution.py:12
  471.6 4.5 copy-start.4
  471.6 6.3 %copy-start.1 = (bf16[128,2880]{0,1:T(8,128)(2,1)S(1)}, bf16[128,2880]{0,1:T(8,128)(2,1)}, u32[]{:S(2)}) copy-start(bf16[128,2880]{0,1:T(8,128)(2,1)} %all-reduce.2.cloned.1.call-done) | copy-start | bytes 2211844
  471.6 58.6 %all-to-all-start.1 = ((bf16[8,16,12,720]{3,1,2,0:T(8,128)(2,1)}), bf16[8,16,12,720]{3,1,2,0:T(8,128)(2,1)S(1)}, u32[]{:S(2)}, u32[]{:S(2)}) async-start(bf16[8,16,12,720]{3,1,2,0:T(8,128)(2,1)} %copy.101), calls=%async_computation.1 | async-start | bytes 4718592 | tf_op jit(solution)/shard_map/all_to_all | solution.py:154
Sparse Core Ops, SparseCore 0:
  8.9 63.7 all-gather.1
  76.7 33.2 all-reduce.1
